TPU v7x, 32 devices: a whole 2x2x4 slice. The times are simulated.
32 devices in a mesh: dp: 8 (over y, x, core), mp: 4 (over z).
Axes of the slice: x: 2, y: 2, z: 4, core: 2. Of those that a mesh axis runs over, the one named last changes fastest.
Arguments:
- tokens: bfloat16 [128, 542, 768], P(('dp', 'mp')), may hold values from -6 to 6
- cotangent: bfloat16 [128, 542, 768], P(('dp', 'mp')), may hold values from -6 to 6
- kept_index: int32 [128, 268], P(('dp', 'mp')), may hold values from 0 to 541, as said below
- attention_weights: float32 [768, 3072], P(None, ('dp', 'mp')), may hold values from -0.4082483 to 0.4082483
- attention_first: float32 [768, 3072], P(None, ('dp', 'mp')), may hold values from -224 to 224
- attention_second: float32 [768, 3072], P(None, ('dp', 'mp')), may hold values from 1372.16 to 5488.64
- attention_average: float32 [768, 3072], P(None, ('dp', 'mp')), may hold values from -0.4082483 to 0.4082483
- feedforward_weights: float32 [2, 768, 3072], P(None, 'dp', 'mp'), may hold values from -0.14433757 to 0.14433757
- feedforward_first: float32 [2, 768, 3072], P(None, 'dp', 'mp'), may hold values from -448 to 448
- feedforward_second: float32 [2, 768, 3072], P(None, 'dp', 'mp'), may hold values from 5488.64 to 21954.56
- feedforward_average: float32 [2, 768, 3072], P(None, 'dp', 'mp'), may hold values from -0.14433757 to 0.14433757
- vector_weights: float32 [13, 768], replicated, may hold values from -1.2 to 1.3
- vector_first: float32 [13, 768], replicated, may hold values from -1024 to 1024
- vector_second: float32 [13, 768], replicated, may hold values from 34304 to 137216
- vector_average: float32 [13, 768], replicated, may hold values from -1.2 to 1.3
Outputs:
- block_output: bfloat16 [128, 542, 768], P(('dp', 'mp'))
- input_gradient: float32 [128, 542, 768], P(('dp', 'mp'))
- attention_gradient: float32 [768, 3072], P(None, ('dp', 'mp'))
- attention_first_new: float32 [768, 3072], P(None, ('dp', 'mp'))
- attention_second_new: float32 [768, 3072], P(None, ('dp', 'mp'))
- attention_weights_new: float32 [768, 3072], P(None, ('dp', 'mp'))
- attention_average_new: float32 [768, 3072], P(None, ('dp', 'mp'))
- attention_copy: bfloat16 [768, 3072], P(None, ('dp', 'mp'))
- feedforward_gradient: float32 [2, 768, 3072], P(None, 'dp', 'mp')
- feedforward_first_new: float32 [2, 768, 3072], P(None, 'dp', 'mp')
- feedforward_second_new: float32 [2, 768, 3072], P(None, 'dp', 'mp')
- feedforward_weights_new: float32 [2, 768, 3072], P(None, 'dp', 'mp')
- feedforward_average_new: float32 [2, 768, 3072], P(None, 'dp', 'mp')
- feedforward_copy: bfloat16 [2, 768, 3072], P(None, 'dp', 'mp')
- vector_gradient: float32 [13, 768], replicated
- vector_first_new: float32 [13, 768], replicated
- vector_second_new: float32 [13, 768], replicated
- vector_weights_new: float32 [13, 768], replicated
- vector_average_new: float32 [13, 768], replicated
- query_bias_gradient: float32 [768], replicated
Inputs may be any that keep to these rules, and one draw needn't show every extreme that they name: `kept_index`: for each image and each of its six crops in order, 197//2 (global crops) or 37//2 (local crops) distinct increasing positions inside that crop; the crop's first and last positions are always among them.
All inputs are finite; a program needn't handle non-finite values.
Results may differ from a plain program's by a relative error of at most 0.0098.
The roundings to bfloat16 on the way count: a program that leaves them out, or rounds other values in their place, can miss the bound.
Values may be sent and summed in bfloat16 or wider, within the bound.
A program may use at most 192 MiB of HBM per device.

v0:
```python
import jax
import jax.numpy as jnp
import numpy as np
from jax import lax
from jax.sharding import PartitionSpec as P

H = 12
HD = 64
FF = 3072
LG = 197
LL = 37
HIGHEST = lax.Precision.HIGHEST


def crop_labels():
    labels = [0] * (LG // 2) + [1] * (LG // 2)
    for crop in range(2, 6):
        labels = labels + [crop] * (LL // 2)
    return np.array(labels, np.int32)


def normalize(rows):
    center = rows - jnp.mean(rows, axis=-1, keepdims=True)
    spread = jnp.mean(center * center, axis=-1, keepdims=True)
    inverse = lax.rsqrt(spread + 1e-06)
    return (center * inverse, inverse)


def norm_backward(upstream, standard, inverse, gain):
    scaled = upstream * gain
    return inverse * (
        scaled
        - jnp.mean(scaled, axis=-1, keepdims=True)
        - standard * jnp.mean(scaled * standard, axis=-1, keepdims=True)
    )


def gelu_slope(inner):
    return (
        0.5 * (1.0 + lax.erf(inner * 0.7071067811865476))
        + inner * jnp.exp(-0.5 * inner * inner) * 0.3989422804014327
    )


def transpose_product(left, right):
    return lax.dot_general(
        left, right, (((0,), (0,)), ((), ())), preferred_element_type=jnp.float32
    )


def product_transposed(left, right):
    return lax.dot_general(
        left, right, (((1,), (1,)), ((), ())), preferred_element_type=jnp.float32
    )


def adamw(grad, first, second, master, average, rate, decay):
    first_new = 0.5 * first + 0.5 * grad
    second_new = 0.5 * second + 0.5 * grad * grad
    update = first_new / (jnp.sqrt(second_new) + 1e-08)
    master_new = master - rate * (update + decay * master)
    average_new = 0.9 * average + 0.1 * master_new
    return (first_new, second_new, master_new, average_new)


def per_device(
    tokens,
    cotangent,
    kept_index,
    attention_weights,
    attention_first,
    attention_second,
    attention_average,
    feedforward_weights,
    feedforward_first,
    feedforward_second,
    feedforward_average,
    vector_weights,
    vector_first,
    vector_second,
    vector_average,
):
    images, length = kept_index.shape
    width = tokens.shape[2]
    heads = H
    head_size = HD
    hidden = FF
    hidden_local = feedforward_weights.shape[2]
    rows_count = images * length
    labels = crop_labels()
    same_crop = jnp.asarray(labels[:, None] == labels[None, :])
    factor = head_size ** (-0.5)
    bf16 = jnp.bfloat16
    f32 = jnp.float32
    attention_full = lax.all_gather(
        attention_weights.astype(bf16), ("dp", "mp"), axis=1, tiled=True
    )
    feed_rows = lax.all_gather(feedforward_weights.astype(bf16), "dp", axis=1, tiled=True)
    first_bias = vector_weights[9:].reshape(hidden)
    bias_used = lax.dynamic_slice_in_dim(
        first_bias, lax.axis_index("mp") * hidden_local, hidden_local
    )
    tokens_float = tokens.astype(f32)
    kept_rows = jnp.take_along_axis(tokens_float, kept_index[:, :, None], axis=1).reshape(
        rows_count, width
    )
    standard_one, inverse_one = normalize(kept_rows)
    normed = (standard_one * vector_weights[0] + vector_weights[1]).astype(bf16)
    normed_float = normed.astype(f32)
    score = jax.nn.sigmoid(jnp.dot(normed_float, vector_weights[2], precision=HIGHEST))
    bias_three = jnp.concatenate(
        [vector_weights[3], jnp.zeros_like(vector_weights[3]), vector_weights[4]]
    )
    project = (
        jnp.dot(normed, attention_full[:, : 3 * width], preferred_element_type=f32) + bias_three
    ).astype(bf16)
    query = project[:, :width].reshape(images, length, heads, head_size)
    keys = project[:, width : 2 * width].reshape(images, length, heads, head_size)
    values = project[:, 2 * width :].reshape(images, length, heads, head_size)
    scores = factor * jnp.einsum("ikhd,ijhd->ihkj", query, keys, preferred_element_type=f32)
    scores = jnp.where(same_crop, scores, -1000000000.0)
    total = jax.nn.logsumexp(scores, axis=-1, keepdims=True)
    probs_low = jnp.exp(scores - total).astype(bf16)
    mixed = (
        jnp.einsum("ihkj,ijhd->ikhd", probs_low, values, preferred_element_type=f32)
        .reshape(rows_count, width)
        .astype(bf16)
    )
    branch = (
        jnp.dot(mixed, attention_full[:, 3 * width :], preferred_element_type=f32)
        + vector_weights[5]
    )
    residual = kept_rows + score[:, None] * branch
    standard_two, inverse_two = normalize(residual)
    normed_two = (standard_two * vector_weights[6] + vector_weights[7]).astype(bf16)
    rows_all = lax.all_gather(normed_two, "mp", axis=0, tiled=True)
    inner = jnp.dot(rows_all, feed_rows[0], preferred_element_type=f32) + bias_used
    activated = jax.nn.gelu(inner, approximate=False).astype(bf16)
    piece = activated
    output = lax.psum_scatter(
        product_transposed(piece, feed_rows[1]).astype(jnp.bfloat16),
        "mp",
        scatter_dimension=0,
        tiled=True,
    ).astype(jnp.float32)
    result = residual + output + vector_weights[8]
    image_index = jnp.arange(images)[:, None]
    block_output = tokens.at[image_index, kept_index].set(
        result.reshape(images, length, width).astype(bf16)
    )
    cot_float = cotangent.astype(f32)
    cot_kept = jnp.take_along_axis(cotangent, kept_index[:, :, None], axis=1).reshape(
        rows_count, width
    )
    cot_all = lax.all_gather(cot_kept, "mp", axis=0, tiled=True)
    down_grad = transpose_product(cot_all, activated)
    active_grad = jnp.dot(cot_all, feed_rows[1], preferred_element_type=f32)
    inner_grad = (active_grad * gelu_slope(inner)).astype(bf16)
    up_grad = transpose_product(rows_all, inner_grad)
    bias_grad_local = jnp.sum(inner_grad.astype(f32), axis=0)
    piece = inner_grad
    normed_two_grad = lax.psum_scatter(
        product_transposed(piece, feed_rows[0]), "mp", scatter_dimension=0, tiled=True
    )
    cot_rows = cot_kept.astype(f32)
    residual_grad = cot_rows + norm_backward(
        normed_two_grad, standard_two, inverse_two, vector_weights[6]
    )
    gain_two_grad = jnp.sum(normed_two_grad * standard_two, axis=0)
    shift_two_grad = jnp.sum(normed_two_grad, axis=0)
    second_bias_grad = jnp.sum(cot_rows, axis=0)
    branch_grad = (score[:, None] * residual_grad).astype(bf16)
    router_grad = jnp.sum(residual_grad * branch, axis=1) * score * (1.0 - score)
    router_weight_grad = jnp.dot(router_grad, normed_float, precision=HIGHEST)
    out_grad = transpose_product(mixed, branch_grad)
    out_bias_grad = jnp.sum(branch_grad.astype(f32), axis=0)
    mixed_grad = product_transposed(branch_grad, attention_full[:, 3 * width :]).astype(bf16)
    mixed_grad = mixed_grad.reshape(images, length, heads, head_size)
    scores_again = factor * jnp.einsum("ikhd,ijhd->ihkj", query, keys, preferred_element_type=f32)
    probs = jnp.exp(jnp.where(same_crop, scores_again, -1000000000.0) - total)
    probs_grad = jnp.einsum("ikhd,ijhd->ihkj", mixed_grad, values, preferred_element_type=f32)
    inner_sum = jnp.sum(probs * probs_grad, axis=-1, keepdims=True)
    scores_grad = (probs * (probs_grad - inner_sum)).astype(bf16)
    query_grad = factor * jnp.einsum(
        "ihkj,ijhd->ikhd", scores_grad, keys, preferred_element_type=f32
    )
    key_grad = factor * jnp.einsum(
        "ihkj,ikhd->ijhd", scores_grad, query, preferred_element_type=f32
    )
    value_grad = jnp.einsum("ihkj,ikhd->ijhd", probs_low, mixed_grad, preferred_element_type=f32)
    project_grad = jnp.concatenate(
        [
            query_grad.reshape(rows_count, width),
            key_grad.reshape(rows_count, width),
            value_grad.reshape(rows_count, width),
        ],
        axis=1,
    ).astype(bf16)
    in_grad = transpose_product(normed, project_grad)
    project_float = project_grad.astype(f32)
    query_bias_grad = jnp.sum(project_float[:, :width], axis=0)
    value_bias_grad = jnp.sum(project_float[:, 2 * width :], axis=0)
    normed_grad = router_grad[:, None] * vector_weights[2] + product_transposed(
        project_grad, attention_full[:, : 3 * width]
    )
    gain_one_grad = jnp.sum(normed_grad * standard_one, axis=0)
    shift_one_grad = jnp.sum(normed_grad, axis=0)
    kept_grad = residual_grad + norm_backward(
        normed_grad, standard_one, inverse_one, vector_weights[0]
    )
    input_gradient = cot_float.at[image_index, kept_index].set(
        kept_grad.reshape(images, length, width)
    )
    attention_local = jnp.concatenate([in_grad, out_grad], axis=1)
    attention_gradient = lax.psum_scatter(
        attention_local, ("dp", "mp"), scatter_dimension=1, tiled=True
    )
    feed_local = jnp.stack([up_grad, down_grad])
    bias_full = lax.dynamic_update_slice_in_dim(
        jnp.zeros((hidden,), f32), bias_grad_local, lax.axis_index("mp") * hidden_local, 0
    )
    feedforward_gradient = lax.psum_scatter(feed_local, "dp", scatter_dimension=1, tiled=True)
    vector_local = jnp.concatenate(
        [
            jnp.stack(
                [
                    gain_one_grad,
                    shift_one_grad,
                    router_weight_grad,
                    query_bias_grad,
                    value_bias_grad,
                    out_bias_grad,
                    gain_two_grad,
                    shift_two_grad,
                    second_bias_grad,
                ]
            ),
            bias_full.reshape(-1, width),
        ],
        axis=0,
    )
    vector_gradient = lax.psum(vector_local, ("dp", "mp"))
    attention_new = adamw(
        attention_gradient,
        attention_first,
        attention_second,
        attention_weights,
        attention_average,
        0.02,
        0.05,
    )
    feedforward_new = adamw(
        feedforward_gradient,
        feedforward_first,
        feedforward_second,
        feedforward_weights,
        feedforward_average,
        0.02,
        0.05,
    )
    vector_new = adamw(
        vector_gradient, vector_first, vector_second, vector_weights, vector_average, 0.2, 0.0
    )
    return (
        block_output,
        input_gradient,
        attention_gradient,
        attention_new[0],
        attention_new[1],
        attention_new[2],
        attention_new[3],
        attention_new[2].astype(bf16),
        feedforward_gradient,
        feedforward_new[0],
        feedforward_new[1],
        feedforward_new[2],
        feedforward_new[3],
        feedforward_new[2].astype(bf16),
        vector_gradient,
        vector_new[0],
        vector_new[1],
        vector_new[2],
        vector_new[3],
        vector_gradient[3],
    )


def solution(mesh):
    in_specs = (
        P(("dp", "mp"), None, None),
        P(("dp", "mp"), None, None),
        P(("dp", "mp"), None),
        P(None, ("dp", "mp")),
        P(None, ("dp", "mp")),
        P(None, ("dp", "mp")),
        P(None, ("dp", "mp")),
        P(None, "dp", "mp"),
        P(None, "dp", "mp"),
        P(None, "dp", "mp"),
        P(None, "dp", "mp"),
        P(),
        P(),
        P(),
        P(),
    )
    out_specs = (
        P(("dp", "mp"), None, None),
        P(("dp", "mp"), None, None),
        P(None, ("dp", "mp")),
        P(None, ("dp", "mp")),
        P(None, ("dp", "mp")),
        P(None, ("dp", "mp")),
        P(None, ("dp", "mp")),
        P(None, ("dp", "mp")),
        P(None, "dp", "mp"),
        P(None, "dp", "mp"),
        P(None, "dp", "mp"),
        P(None, "dp", "mp"),
        P(None, "dp", "mp"),
        P(None, "dp", "mp"),
        P(),
        P(),
        P(),
        P(),
        P(),
        P(),
    )
    return jax.shard_map(
        per_device, mesh=mesh, in_specs=in_specs, out_specs=out_specs, check_vma=False
    )
```

profile of v0, /device:TPU:0, one launch (start us, length us, event | category | flops | bytes accessed | tf_op | source)
XLA Modules:
  0.0 996.7 jit_solution(14015516016372770413)
XLA Ops:
  14.1 18.3 %gather_fusion.1 = bf16[1072,768]{1,0:T(8,128)(2,1)S(1)} fusion(bf16[4,542,768]{2,0,1:T(4,128)(2,1)} %param.17, s32[1072]{0:T(1024)S(1)} %reshape.324), kind=kCustom, calls=%fused_computation.1 | custom fusion | bytes 3301760 | tf_op jit(solution)/shard_map/jit(take_along_axis)/gather | solution.py:152
  39.8 16.3 %gather_fusion = f32[1072,768]{1,0:T(8,128)S(1)} fusion(f32[4,542,768]{2,0,1:T(4,128)} %convert_element_type.94, s32[1072]{0:T(1024)S(1)} %reshape.324), kind=kCustom, calls=%fused_computation | custom fusion | bytes 6594944 | tf_op jit(solution)/shard_map/jit(take_along_axis)/gather | solution.py:104
  112.8 12.7 %fusion = (f32[4,12,268]{2,1,0:T(8,128)S(1)}, f32[4,12,268,268]{2,3,1,0:T(8,128)}) fusion(pred[268,268]{0,1:T(8,128)(4,1)S(1)} %copy-done.18, bf16[4,268,12,64]{1,3,2,0:T(8,128)(2,1)} %copy.127, bf16[4,268,12,64]{1,3,2,0:T(8,128)(2,1)} %copy.128), kind=kOutput, calls=%fused_computation.11 | convolution fusion | flops 451616448 | bytes 17206672 | tf_op jit(solution)/shard_map/ikhd,ijhd->ihkj/dot_general | solution.py:120
  126.2 12.0 %exponential_reduce_fusion = f32[4,12,268]{2,1,0:T(8,128)} fusion(f32[4,12,268,268]{2,3,1,0:T(8,128)} %get-tuple-element.142, f32[4,12,268]{2,1,0:T(8,128)} %is-finite_select_fusion, pred[268,268]{0,1:T(8,128)(4,1)S(1)} %copy-done.18), kind=kLoop, calls=%fused_computation.7 | loop fusion | flops 13777344 | bytes 13964944 | tf_op jit(solution)/shard_map/reduce_sum | solution.py:122
  152.6 12.4 %convert_bitcast_fusion.2 = bf16[4,268,12,64]{1,3,2,0:T(8,128)(2,1)S(1)} fusion(bf16[4,268,12,64]{1,3,2,0:T(8,128)(2,1)} %copy.129, f32[4,12,268,268]{2,3,1,0:T(8,128)} %get-tuple-element.142, f32[4,12,268]{2,1,0:T(8,128)S(1)} %log_add_fusion, pred[268,268]{0,1:T(8,128)(4,1)S(1)} %copy-done.18), kind=kOutput, calls=%fused_computation.84 | convolution fusion | flops 455900160 | bytes 17206672 | tf_op jit(solution)/shard_map/ihkj,ijhd->ikhd/dot_general | solution.py:125
  184.0 119.6 %all-gather.7.cloned.1.call-done = bf16[4288,768]{1,0:T(8,128)(2,1)} async-done(((bf16[1072,768]{1,0:T(8,128)(2,1)}), bf16[4288,768]{1,0:T(8,128)(2,1)}) %all-gather.7.cloned.1.call-update) | async-done | bytes 6586384 | tf_op jit(solution)/shard_map/all_gather | solution.py:136
  303.6 38.0 %fusion.3 = (bf16[4288,768]{1,0:T(8,128)(2,1)}, f32[4288,768]{1,0:T(8,128)}) fusion(f32[768]{0:T(1024)S(1)} %dynamic_slice.3, bf16[4288,768]{1,0:T(8,128)(2,1)} %all-gather.7.cloned.1.call-done, bf16[2,768,768]{2,1,0:T(8,128)(2,1)} %all-gather.9.cloned.1.call-done), kind=kOutput, calls=%fused_computation.15 | convolution fusion | flops 5275680768 | bytes 27528192 | tf_op jit(solution)/shard_map/dot_general | solution.py:137
  341.6 81.8 %all-gather.11.cloned.1.call-done = bf16[4288,768]{1,0:T(8,128)(2,1)} async-done(((bf16[1072,768]{1,0:T(8,128)(2,1)}), bf16[4288,768]{1,0:T(8,128)(2,1)}) %all-gather.11.cloned.1.call-update) | async-done | bytes 6586384 | tf_op jit(solution)/shard_map/all_gather | solution.py:155
  423.4 11.5 %convert_reduce_fusion = (f32[768]{0:T(1024)S(1)}, bf16[4288,768]{1,0:T(8,128)(2,1)S(1)}) fusion(f32[4288,768]{1,0:T(8,128)} %get-tuple-element.145, f32[768]{0:T(1024)S(1)} %dynamic_slice.3, bf16[4288,768]{1,0:T(8,128)(2,1)} %all-gather.11.cloned.1.call-done, bf16[2,768,768]{2,1,0:T(8,128)(2,1)S(1)} %copy-done.64), kind=kOutput, calls=%fused_computation.22 | convolution fusion | flops 5101140992 | bytes 27532288 | tf_op jit(solution)/shard_map/dot_general | solution.py:157
  437.6 8.5 fusion.36
  446.2 9.7 convolution_bitcast_fusion.1
  455.9 9.5 convolution_bitcast_fusion
  467.9 10.1 %convolution_convert_fusion = bf16[4288,768]{1,0:T(8,128)(2,1)} fusion(bf16[4288,768]{1,0:T(8,128)(2,1)} %get-tuple-element.144, bf16[2,768,768]{2,1,0:T(8,128)(2,1)S(1)} %copy-done.64), kind=kOutput, calls=%fused_computation.41 | convolution fusion | flops 5061623808 | bytes 14352384 | tf_op jit(solution)/shard_map/dot_general | solution.py:52
  478.1 187.8 %reduce-scatter.9.cloned.1.call-done = f32[1072,768]{1,0:T(8,128)} async-done(((f32[4288,768]{1,0:T(8,128)}), f32[1072,768]{1,0:T(8,128)}) %reduce-scatter.9.cloned.1.call-update) | async-done | bytes 3293200 | tf_op jit(solution)/shard_map/reduce_scatter | solution.py:162
  691.3 14.5 %convert_bitcast_fusion.1 = bf16[4,268,12,64]{1,3,2,0:T(8,128)(2,1)} fusion(bf16[4,268,12,64]{1,3,2,0:T(8,128)(2,1)} %copy.133, f32[4,12,268,268]{2,3,1,0:T(8,128)} %get-tuple-element.142, f32[4,12,268]{2,1,0:T(8,128)S(1)} %copy-done.26, pred[268,268]{0,1:T(8,128)(4,1)S(1)} %copy-done.19), kind=kOutput, calls=%fused_computation.83 | convolution fusion | flops 455900160 | bytes 17206672 | tf_op jit(solution)/shard_map/ihkj,ikhd->ijhd/dot_general | solution.py:190
  715.6 15.3 %multiply_reduce_fusion = (f32[4,12,268]{2,1,0:T(8,128)S(1)}, f32[4,12,268,268]{2,3,1,0:T(8,128)}) fusion(f32[4,12,268,268]{2,3,1,0:T(8,128)} %get-tuple-element.142, f32[4,12,268]{2,1,0:T(8,128)S(1)} %copy-done.26, pred[268,268]{0,1:T(8,128)(4,1)S(1)} %copy-done.19, bf16[4,268,12,64]{1,3,2,0:T(8,128)(2,1)} %copy.133, bf16[4,268,12,64]{1,3,2,0:T(8,128)(2,1)} %copy.129), kind=kOutput, calls=%fused_computation.5 | convolution fusion | flops 458511552 | bytes 31048336 | tf_op jit(solution)/shard_map/ikhd,ijhd->ihkj/dot_general | solution.py:181
  730.8 15.8 %multiply_convert_fusion = bf16[4,12,268,268]{2,3,1,0:T(8,128)(2,1)S(1)} fusion(f32[4,12,268,268]{2,3,1,0:T(8,128)} %get-tuple-element.147, f32[4,12,268,268]{2,3,1,0:T(8,128)} %get-tuple-element.142, f32[4,12,268]{2,1,0:T(8,128)S(1)} %get-tuple-element.146, f32[4,12,268]{2,1,0:T(8,128)S(1)} %copy-done.26, pred[268,268]{0,1:T(8,128)(4,1)S(1)} %copy-done.19), kind=kLoop, calls=%fused_computation.4 | loop fusion | flops 20685312 | bytes 34650256 | tf_op jit(solution)/shard_map/convert_element_type | solution.py:183
  789.0 8.7 pad_maximum_fusion
  797.7 9.6 copy.153
  842.7 13.8 %scatter_custom_fusion = bf16[2168,768]{1,0:T(8,128)(2,1)} fusion(bf16[2168,768]{1,0:T(8,128)(2,1)} %reshape.317, s32[1072]{0:T(1024)S(1)} %reshape.336, f32[1072,768]{1,0:T(8,128)S(1)} %copy-done.2, bf16[1072,768]{1,0:T(8,128)(2,1)} %reduce-scatter.7.cloned.1.call-done, f32[768]{0:T(1024)S(1)} %copy-done.58), kind=kCustom, calls=%fused_computation.87 | custom fusion | flops 3293184 | bytes 8273920
  873.5 10.7 %multiply_reduce_fusion.3 = (f32[768]{0:T(1024)S(1)}, f32[1072]{0:T(1024)S(1)}, f32[1072]{0:T(1024)S(1)}, f32[768]{0:T(1024)S(1)}, f32[1072,768]{1,0:T(8,128)}) fusion(f32[1072]{0:T(1024)S(1)} %copy-done.41, f32[1072]{0:T(1024)S(1)} %copy-done.39, f32[1072,768]{1,0:T(8,128)S(1)} %copy-done.4, pred[1072]{0:T(1024)(128)(4,1)S(1)} %copy-done.48, ...), kind=kOutput, calls=%fused_computation.56 | convolution fusion | flops 3803623936 | bytes 15468528 | tf_op jit(solution)/shard_map/dot_general | solution.py:52
  884.3 17.0 %scatter_custom_fusion.1 = f32[2168,768]{1,0:T(8,128)} fusion(f32[2168,768]{1,0:T(8,128)} %reshape.321, s32[1072]{0:T(1024)S(1)} %reshape.336, f32[1072,768]{1,0:T(8,128)} %get-tuple-element.127, f32[1072,768]{1,0:T(8,128)} %get-tuple-element.148, f32[1072]{0:T(1024)S(1)} %broadcast_multiply_fusion, f32[1072]{0:T(1024)S(1)} %broadcast_multiply_fusion.1, ...), kind=kCustom, calls=%fused_computation.57 | custom fusion | flops 7409664 | bytes 16578560
  914.2 41.2 %psum.7 = f32[13,768]{1,0:T(8,128)S(1)} all-reduce(f32[13,768]{1,0:T(8,128)S(1)} %concatenate.21), channel_id=1, replica_groups=mesh['dp'=8,'mp'=4] {'dp','mp'}, use_global_device_ids=true, to_apply=%region_27.28 | all-reduce | flops 9984 | bytes 79872 | tf_op jit(solution)/shard_map/psum | solution.py:242
  956.7 30.2 %reduce-scatter.13.cloned.1.call-done = f32[96,768]{1,0:T(8,128)} async-done(((f32[3072,768]{1,0:T(8,128)}), f32[96,768]{1,0:T(8,128)}) %reduce-scatter.13.cloned.1.call-update) | async-done | bytes 294928
  (253 shorter events, 256.5 us)
Async XLA Ops:
  7.2 70.5 %all-gather.5.cloned.1.call-start = ((), (), s32[]{:S(2)}) async-start(), calls=%async_computation.4 | async-start | bytes 4866048 | tf_op jit(solution)/shard_map/all_gather | solution.py:95
  8.9 175.1 %all-gather.9.cloned.1.call-start = ((), (), s32[]{:S(2)}) async-start(), calls=%async_computation.6 | async-start | bytes 2654208 | tf_op jit(solution)/shard_map/all_gather | solution.py:98
  10.8 292.8 %all-gather.7.cloned.1.call-start = ((), (), s32[]{:S(2)}) async-start(), calls=%async_computation.5 | async-start | bytes 8232960 | tf_op jit(solution)/shard_map/all_gather | solution.py:136
  12.3 61.4 %copy-start.46 = (pred[1072]{0:T(1024)(128)(4,1)}, pred[1072]{0:T(1024)(128)(4,1)S(1)}, u32[]{:S(2)}) copy-start(pred[1072]{0:T(1024)(128)(4,1)S(1)} %broadcast_in_dim.74) | copy-start | bytes 3220
  14.1 59.6 %copy-start.51 = (f32[768]{0:T(1024)}, f32[768]{0:T(1024)S(1)}, u32[]{:S(2)}) copy-start(f32[768]{0:T(1024)S(1)} %get-tuple-element.117) | copy-start | bytes 9220
  56.1 116.9 %copy-start.3 = (f32[1072,768]{1,0:T(8,128)}, f32[1072,768]{1,0:T(8,128)S(1)}, u32[]{:S(2)}) copy-start(f32[1072,768]{1,0:T(8,128)S(1)} %gather_fusion) | copy-start | bytes 9879556
  73.7 99.3 %copy-start.44 = (f32[1072]{0:T(1024)}, f32[1072]{0:T(1024)S(1)}, u32[]{:S(2)}) copy-start(f32[1072]{0:T(1024)S(1)} %add_divide_fusion) | copy-start | bytes 12868
  182.3 241.1 %all-gather.11.cloned.1.call-start = ((), (), s32[]{:S(2)}) async-start(), calls=%async_computation.8 | async-start | bytes 8232960 | tf_op jit(solution)/shard_map/all_gather | solution.py:155
  183.8 482.1 %reduce-scatter.9.cloned.1.call-start = ((), (), s32[]{:S(2)}) async-start(), calls=%async_computation.9 | async-start | bytes 16465920 | tf_op jit(solution)/shard_map/reduce_scatter | solution.py:162
  184.0 239.4 %copy-start.64 = (bf16[2,768,768]{2,1,0:T(8,128)(2,1)S(1)}, bf16[2,768,768]{2,1,0:T(8,128)(2,1)}, u32[]{:S(2)}) copy-start(bf16[2,768,768]{2,1,0:T(8,128)(2,1)} %all-gather.9.cloned.1.call-done) | copy-start | bytes 7077892
  446.1 383.5 %reduce-scatter.11.cloned.1.call-start = ((), (), s32[]{:S(2)}) async-start(), calls=%async_computation.10 | async-start | bytes 5308416 | tf_op jit(solution)/shard_map/reduce_scatter | solution.py:222
  467.9 374.8 %reduce-scatter.7.cloned.1.call-start = ((), (), s32[]{:S(2)}) async-start(), calls=%async_computation.7 | async-start | bytes 8232960 | tf_op jit(solution)/shard_map/reduce_scatter | solution.py:140
  478.0 187.9 %copy-start.2 = (f32[1072,768]{1,0:T(8,128)S(1)}, f32[1072,768]{1,0:T(8,128)}, u32[]{:S(2)}) copy-start(f32[1072,768]{1,0:T(8,128)} %copy-done.1) | copy-start | bytes 9879556
  478.0 187.9 %copy-start.35 = (f32[1072]{0:T(1024)S(1)}, f32[1072]{0:T(1024)}, u32[]{:S(2)}) copy-start(f32[1072]{0:T(1024)} %copy-done.34) | copy-start | bytes 12868
  478.0 187.9 %copy-start.37 = (f32[1072]{0:T(1024)S(1)}, f32[1072]{0:T(1024)}, u32[]{:S(2)}) copy-start(f32[1072]{0:T(1024)} %copy-done.36) | copy-start | bytes 12868
  478.0 187.9 %copy-start.50 = (f32[768]{0:T(1024)S(1)}, f32[768]{0:T(1024)}, u32[]{:S(2)}) copy-start(f32[768]{0:T(1024)} %get-tuple-element.112) | copy-start | bytes 9220
  478.1 191.3 %copy-start.45 = (f32[1072]{0:T(1024)S(1)}, f32[1072]{0:T(1024)}, u32[]{:S(2)}) copy-start(f32[1072]{0:T(1024)} %copy-done.44) | copy-start | bytes 12868
  478.1 191.3 %copy-start.48 = (pred[1072]{0:T(1024)(128)(4,1)S(1)}, pred[1072]{0:T(1024)(128)(4,1)}, u32[]{:S(2)}) copy-start(pred[1072]{0:T(1024)(128)(4,1)} %copy-done.46) | copy-start | bytes 3220
  478.1 508.9 %reduce-scatter.13.cloned.1.call-start = ((), (), s32[]{:S(2)}) async-start(), calls=%async_computation.11 | async-start | bytes 9732096
  909.6 46.4 %copy-start.55 = (f32[13,768]{1,0:T(8,128)S(1)}, f32[13,768]{1,0:T(8,128)}, u32[]{:S(2)}) copy-start(f32[13,768]{1,0:T(8,128)} %param.29) | copy-start | bytes 119812
  909.7 77.3 %copy-start.24 = (f32[768,96]{0,1:T(8,128)S(1)}, f32[768,96]{0,1:T(8,128)}, u32[]{:S(2)}) copy-start(f32[768,96]{0,1:T(8,128)} %param.19) | copy-start | bytes 884740
  909.7 77.3 %copy-start.28 = (f32[768,96]{0,1:T(8,128)S(1)}, f32[768,96]{0,1:T(8,128)}, u32[]{:S(2)}) copy-start(f32[768,96]{0,1:T(8,128)} %param.21) | copy-start | bytes 884740
  909.7 77.3 %copy-start.29 = (f32[768,96]{0,1:T(8,128)S(1)}, f32[768,96]{0,1:T(8,128)}, u32[]{:S(2)}) copy-start(f32[768,96]{0,1:T(8,128)} %param.20) | copy-start | bytes 884740
  913.3 75.6 %copy-start.30 = (f32[768,96]{0,1:T(8,128)S(1)}, f32[768,96]{0,1:T(8,128)}, u32[]{:S(2)}) copy-start(f32[768,96]{0,1:T(8,128)} %param.22) | copy-start | bytes 884740
  (50 other events, 377.3 us)
Sparse Core Ops, SparseCore 0:
  11.4 66.2 all-gather.4
  80.2 27.8 all-gather.8
  182.4 121.1 all-gather.6
  305.0 118.3 all-gather.10
  446.3 219.5 reduce-scatter.8
  669.8 54.9 reduce-scatter.10
  727.2 115.4 reduce-scatter.6
  850.2 136.7 reduce-scatter.12
where the time goes:
time: 1010 us; the launch traced here: 997 us
  waiting for transfers between devices  430 us (43%)
  matrix products  194 us (19%)
  local copies, waits for them, and re-layouts  187 us (19%)
  other arithmetic  130 us (13%)
  blocking collectives  41.2 us (4%)
  between operations  15.1 us (1%)
    reduce_scatter x1, waiting for transfers between devices, per_device(): lax.psum_scatter(product_transposed(piece, feed_rows[0]), 'mp', scatter_d...  188 us
    all_gather x1, waiting for transfers between devices, per_device(): rows_all = lax.all_gather(normed_two, 'mp', axis=0, tiled=True)  120 us
    all_gather x1, waiting for transfers between devices, per_device(): cot_all = lax.all_gather(cot_kept, 'mp', axis=0, tiled=True)  81.8 us
    unnamed x140, local copies, waits for them, and re-layouts  53.9 us
    psum x1, blocking collectives, per_device(): vector_gradient = lax.psum(vector_local, ('dp', 'mp'))  41.2 us
    dot_general x1, matrix products, per_device(): jnp.dot(rows_all, feed_rows[0], preferred_element_type=f32) + bias_used  38 us
    unnamed x6, other arithmetic  36.7 us
    dot_general x4, matrix products, product_transposed(): lax.dot_general(left, right, (((1,), (1,)), ((), ())), preferred_element_...  33.3 us
  transfers between devices with their start and end apart: 8, of which 6 were waited for; matrix products, arithmetic and copies ran while one was open for 48% of the time, Pallas kernels for 0%

commit v1 on v0

--- a/solution.py
+++ b/solution.py
@@ -239,7 +239,7 @@
         ],
         axis=0,
     )
-    vector_gradient = lax.psum(vector_local, ("dp", "mp"))
+    vector_gradient = jnp.sum(lax.all_gather(vector_local, ("dp", "mp")), axis=0)
     attention_new = adamw(
         attention_gradient,
         attention_first,

time: 1010 us -> 1060 us (1.050)
  waiting for transfers between devices: 430 us -> 522 us
  blocking collectives: 41.2 us -> 0 us
  local copies, waits for them, and re-layouts: 187 us -> 200 us
  other arithmetic: 130 us -> 118 us
    unnamed x9 -> x10, waiting for transfers between devices: 30.4 us -> 139 us
    psum x1 -> x0, blocking collectives: 41.2 us -> none  [per_device(): vector_gradient = lax.psum(vector_local, ('dp', 'mp'))]
    gather x2, local copies, waits for them, and re-layouts: 18.4 us -> 29.4 us  [per_device(): jnp.take_along_axis(tokens_float, kept_index[:, :, None], axis=1)]
  transfers between devices with their start and end apart: 8 -> 9, of which waited for: 6 -> 5; matrix products, arithmetic and copies ran while one was open for 48% -> 45% of each run, Pallas kernels for 0% -> 0%
where the time goes in v1:
time: 1060 us; the launch traced here: 1050 us
  waiting for transfers between devices  522 us (49%)
  local copies, waits for them, and re-layouts  200 us (19%)
  matrix products  198 us (19%)
  other arithmetic  118 us (11%)
  between operations  14.9 us (1%)
    reduce_scatter x1, waiting for transfers between devices, per_device(): lax.psum_scatter(product_transposed(piece, feed_rows[0]), 'mp', scatter_d...  185 us
    unnamed x10, waiting for transfers between devices  139 us
    all_gather x1, waiting for transfers between devices, per_device(): rows_all = lax.all_gather(normed_two, 'mp', axis=0, tiled=True)  113 us
    all_gather x1, waiting for transfers between devices, per_device(): cot_all = lax.all_gather(cot_kept, 'mp', axis=0, tiled=True)  81.6 us
    unnamed x140, local copies, waits for them, and re-layouts  58.3 us
    dot_general x1, matrix products, per_device(): jnp.dot(rows_all, feed_rows[0], preferred_element_type=f32) + bias_used  38.2 us
    unnamed x6, other arithmetic  36.2 us
    dot_general x4, matrix products, transpose_product(): lax.dot_general(left, right, (((0,), (0,)), ((), ())), preferred_element_...  34.1 us
  transfers between devices with their start and end apart: 9, of which 5 were waited for; matrix products, arithmetic and copies ran while one was open for 45% of the time, Pallas kernels for 0%

profile of v1, /device:TPU:0, one launch (start us, length us, event | category | flops | bytes accessed | tf_op | source)
XLA Modules:
  0.0 1053.6 jit_solution(4181431639071301422)
XLA Ops:
  14.1 23.7 %gather_fusion.1 = bf16[1072,768]{1,0:T(8,128)(2,1)S(1)} fusion(bf16[4,542,768]{2,0,1:T(4,128)(2,1)} %param.17, s32[1072]{0:T(1024)S(1)} %reshape.324), kind=kCustom, calls=%fused_computation.1 | custom fusion | bytes 3301760 | tf_op jit(solution)/shard_map/jit(take_along_axis)/gather | solution.py:152
  45.1 26.1 %gather_fusion = f32[1072,768]{1,0:T(8,128)} fusion(f32[4,542,768]{2,0,1:T(4,128)} %convert_element_type.94, s32[1072]{0:T(1024)S(1)} %reshape.324), kind=kCustom, calls=%fused_computation | custom fusion | bytes 6594944 | tf_op jit(solution)/shard_map/jit(take_along_axis)/gather | solution.py:104
  121.6 12.9 %fusion = (f32[4,12,268]{2,1,0:T(8,128)S(1)}, f32[4,12,268,268]{2,3,1,0:T(8,128)}) fusion(pred[268,268]{0,1:T(8,128)(4,1)S(1)} %copy-done.21, bf16[4,268,12,64]{1,3,2,0:T(8,128)(2,1)S(1)} %copy.127, bf16[4,268,12,64]{1,3,2,0:T(8,128)(2,1)} %copy.128), kind=kOutput, calls=%fused_computation.11 | convolution fusion | flops 451616448 | bytes 17206672 | tf_op jit(solution)/shard_map/ikhd,ijhd->ihkj/dot_general | solution.py:120
  134.5 11.7 %exponential_reduce_fusion = f32[4,12,268]{2,1,0:T(8,128)S(1)} fusion(f32[4,12,268,268]{2,3,1,0:T(8,128)} %get-tuple-element.142, f32[4,12,268]{2,1,0:T(8,128)S(1)} %is-finite_select_fusion, pred[268,268]{0,1:T(8,128)(4,1)S(1)} %copy-done.21), kind=kLoop, calls=%fused_computation.7 | loop fusion | flops 13777344 | bytes 13964944 | tf_op jit(solution)/shard_map/reduce_sum | solution.py:122
  156.5 12.6 %convert_bitcast_fusion.2 = bf16[4,268,12,64]{1,3,2,0:T(8,128)(2,1)S(1)} fusion(bf16[4,268,12,64]{1,3,2,0:T(8,128)(2,1)S(1)} %copy.129, f32[4,12,268,268]{2,3,1,0:T(8,128)} %get-tuple-element.142, f32[4,12,268]{2,1,0:T(8,128)S(1)} %log_add_fusion, pred[268,268]{0,1:T(8,128)(4,1)S(1)} %copy-done.21), kind=kOutput, calls=%fused_computation.84 | convolution fusion | flops 455900160 | bytes 17206672 | tf_op jit(solution)/shard_map/ihkj,ijhd->ikhd/dot_general | solution.py:125
  190.4 113.1 %all-gather.10.cloned.1.call-done = bf16[4288,768]{1,0:T(8,128)(2,1)} async-done(((bf16[1072,768]{1,0:T(8,128)(2,1)}), bf16[4288,768]{1,0:T(8,128)(2,1)}) %all-gather.10.cloned.1.call-update) | async-done | bytes 6586384 | tf_op jit(solution)/shard_map/all_gather | solution.py:136
  303.5 38.2 %fusion.3 = (bf16[4288,768]{1,0:T(8,128)(2,1)}, f32[4288,768]{1,0:T(8,128)}) fusion(f32[768]{0:T(1024)S(1)} %dynamic_slice.3, bf16[4288,768]{1,0:T(8,128)(2,1)} %all-gather.10.cloned.1.call-done, bf16[2,768,768]{2,1,0:T(8,128)(2,1)} %all-gather.12.cloned.1.call-done), kind=kOutput, calls=%fused_computation.15 | convolution fusion | flops 5275680768 | bytes 27528192 | tf_op jit(solution)/shard_map/dot_general | solution.py:137
  341.7 81.6 %all-gather.14.cloned.1.call-done = bf16[4288,768]{1,0:T(8,128)(2,1)} async-done(((bf16[1072,768]{1,0:T(8,128)(2,1)}), bf16[4288,768]{1,0:T(8,128)(2,1)}) %all-gather.14.cloned.1.call-update) | async-done | bytes 6586384 | tf_op jit(solution)/shard_map/all_gather | solution.py:155
  423.3 11.5 %convert_reduce_fusion = (f32[768]{0:T(1024)S(1)}, bf16[4288,768]{1,0:T(8,128)(2,1)S(1)}) fusion(f32[4288,768]{1,0:T(8,128)} %get-tuple-element.145, f32[768]{0:T(1024)S(1)} %dynamic_slice.3, bf16[4288,768]{1,0:T(8,128)(2,1)} %all-gather.14.cloned.1.call-done, bf16[2,768,768]{2,1,0:T(8,128)(2,1)S(1)} %copy-done.63), kind=kOutput, calls=%fused_computation.22 | convolution fusion | flops 5101140992 | bytes 27532288 | tf_op jit(solution)/shard_map/dot_general | solution.py:157
  437.5 8.5 fusion.36
  446.1 9.7 convolution_bitcast_fusion.1
  455.8 9.5 convolution_bitcast_fusion
  469.4 10.1 convolution_convert_fusion
  480.5 185.3 %reduce-scatter.9.cloned.1.call-done = f32[1072,768]{1,0:T(8,128)} async-done(((f32[4288,768]{1,0:T(8,128)}), f32[1072,768]{1,0:T(8,128)}) %reduce-scatter.9.cloned.1.call-update) | async-done | bytes 3293200 | tf_op jit(solution)/shard_map/reduce_scatter | solution.py:162
  690.9 14.5 %convert_bitcast_fusion.1 = bf16[4,268,12,64]{1,3,2,0:T(8,128)(2,1)} fusion(bf16[4,268,12,64]{1,3,2,0:T(8,128)(2,1)} %copy.133, f32[4,12,268,268]{2,3,1,0:T(8,128)} %get-tuple-element.142, f32[4,12,268]{2,1,0:T(8,128)S(1)} %copy-done.28, pred[268,268]{0,1:T(8,128)(4,1)S(1)} %copy-done.22), kind=kOutput, calls=%fused_computation.83 | convolution fusion | flops 455900160 | bytes 17206672 | tf_op jit(solution)/shard_map/ihkj,ikhd->ijhd/dot_general | solution.py:190
  715.0 15.1 %multiply_reduce_fusion = (f32[4,12,268]{2,1,0:T(8,128)S(1)}, f32[4,12,268,268]{2,3,1,0:T(8,128)}) fusion(f32[4,12,268,268]{2,3,1,0:T(8,128)} %get-tuple-element.142, f32[4,12,268]{2,1,0:T(8,128)S(1)} %copy-done.28, pred[268,268]{0,1:T(8,128)(4,1)S(1)} %copy-done.22, bf16[4,268,12,64]{1,3,2,0:T(8,128)(2,1)} %copy.133, bf16[4,268,12,64]{1,3,2,0:T(8,128)(2,1)} %copy-done.13), kind=kOutput, calls=%fused_computation.5 | convolution fusion | flops 458511552 | bytes 31048336 | tf_op jit(solution)/shard_map/ikhd,ijhd->ihkj/dot_general | solution.py:181
  730.1 16.2 %multiply_convert_fusion = bf16[4,12,268,268]{2,3,1,0:T(8,128)(2,1)S(1)} fusion(f32[4,12,268,268]{2,3,1,0:T(8,128)} %get-tuple-element.147, f32[4,12,268,268]{2,3,1,0:T(8,128)} %get-tuple-element.142, f32[4,12,268]{2,1,0:T(8,128)S(1)} %get-tuple-element.146, f32[4,12,268]{2,1,0:T(8,128)S(1)} %copy-done.28, pred[268,268]{0,1:T(8,128)(4,1)S(1)} %copy-done.22), kind=kLoop, calls=%fused_computation.4 | loop fusion | flops 20685312 | bytes 34650256 | tf_op jit(solution)/shard_map/convert_element_type | solution.py:183
  781.2 9.0 multiply_reduce_fusion.3
  798.9 9.7 fusion.59
  808.6 8.8 pad_maximum_fusion
  817.4 9.7 copy.153
  853.3 13.8 %scatter_custom_fusion = bf16[2168,768]{1,0:T(8,128)(2,1)} fusion(bf16[2168,768]{1,0:T(8,128)(2,1)} %reshape.317, s32[1072]{0:T(1024)S(1)} %reshape.336, f32[1072,768]{1,0:T(8,128)S(1)} %copy-done.2, bf16[1072,768]{1,0:T(8,128)(2,1)} %reduce-scatter.7.cloned.1.call-done, f32[768]{0:T(1024)S(1)} %copy-done.58), kind=kCustom, calls=%fused_computation.87 | custom fusion | flops 3293184 | bytes 8273920
  874.2 16.6 %scatter_custom_fusion.1 = f32[2168,768]{1,0:T(8,128)} fusion(f32[2168,768]{1,0:T(8,128)} %reshape.321, s32[1072]{0:T(1024)S(1)} %reshape.336, f32[1072,768]{1,0:T(8,128)} %copy-done.6, f32[1072,768]{1,0:T(8,128)} %get-tuple-element.148, f32[1072]{0:T(1024)S(1)} %broadcast_multiply_fusion, f32[1072]{0:T(1024)S(1)} %broadcast_multiply_fusion.1, ...), kind=kCustom, calls=%fused_computation.57 | custom fusion | flops 7409664 | bytes 16578560
  904.9 139.2 %reduce-scatter.13.cloned.1.call-done = f32[96,768]{1,0:T(8,128)} async-done(((f32[3072,768]{1,0:T(8,128)}), f32[96,768]{1,0:T(8,128)}) %reduce-scatter.13.cloned.1.call-update) | async-done | bytes 294928
  (256 shorter events, 231.6 us)
Async XLA Ops:
  7.2 85.3 %all-gather.8.cloned.1.call-start = ((), (), s32[]{:S(2)}) async-start(), calls=%async_computation.4 | async-start | bytes 4866048 | tf_op jit(solution)/shard_map/all_gather | solution.py:95
  8.9 181.5 %all-gather.12.cloned.1.call-start = ((), (), s32[]{:S(2)}) async-start(), calls=%async_computation.6 | async-start | bytes 2654208 | tf_op jit(solution)/shard_map/all_gather | solution.py:98
  10.8 292.7 %all-gather.10.cloned.1.call-start = ((), (), s32[]{:S(2)}) async-start(), calls=%async_computation.5 | async-start | bytes 8232960 | tf_op jit(solution)/shard_map/all_gather | solution.py:136
  12.3 175.0 %copy-start.48 = (pred[1072]{0:T(1024)(128)(4,1)}, pred[1072]{0:T(1024)(128)(4,1)S(1)}, u32[]{:S(2)}) copy-start(pred[1072]{0:T(1024)(128)(4,1)S(1)} %broadcast_in_dim.74) | copy-start | bytes 3220
  14.1 170.1 %copy-start.50 = (f32[768]{0:T(1024)}, f32[768]{0:T(1024)S(1)}, u32[]{:S(2)}) copy-start(f32[768]{0:T(1024)S(1)} %get-tuple-element.112) | copy-start | bytes 9220
  90.0 87.0 %copy-start.46 = (f32[1072]{0:T(1024)}, f32[1072]{0:T(1024)S(1)}, u32[]{:S(2)}) copy-start(f32[1072]{0:T(1024)S(1)} %add_divide_fusion) | copy-start | bytes 12868
  187.3 236.1 %all-gather.14.cloned.1.call-start = ((), (), s32[]{:S(2)}) async-start(), calls=%async_computation.8 | async-start | bytes 8232960 | tf_op jit(solution)/shard_map/all_gather | solution.py:155
  190.2 475.6 %reduce-scatter.9.cloned.1.call-start = ((), (), s32[]{:S(2)}) async-start(), calls=%async_computation.9 | async-start | bytes 16465920 | tf_op jit(solution)/shard_map/reduce_scatter | solution.py:162
  190.4 233.0 %copy-start.63 = (bf16[2,768,768]{2,1,0:T(8,128)(2,1)S(1)}, bf16[2,768,768]{2,1,0:T(8,128)(2,1)}, u32[]{:S(2)}) copy-start(bf16[2,768,768]{2,1,0:T(8,128)(2,1)} %all-gather.12.cloned.1.call-done) | copy-start | bytes 7077892
  446.0 402.5 %reduce-scatter.11.cloned.1.call-start = ((), (), s32[]{:S(2)}) async-start(), calls=%async_computation.10 | async-start | bytes 5308416 | tf_op jit(solution)/shard_map/reduce_scatter | solution.py:222
  467.7 385.6 %reduce-scatter.7.cloned.1.call-start = ((), (), s32[]{:S(2)}) async-start(), calls=%async_computation.7 | async-start | bytes 8232960 | tf_op jit(solution)/shard_map/reduce_scatter | solution.py:140
  479.5 186.3 %copy-start.2 = (f32[1072,768]{1,0:T(8,128)S(1)}, f32[1072,768]{1,0:T(8,128)}, u32[]{:S(2)}) copy-start(f32[1072,768]{1,0:T(8,128)} %copy-done.1) | copy-start | bytes 9879556
  479.5 186.3 %copy-start.37 = (f32[1072]{0:T(1024)S(1)}, f32[1072]{0:T(1024)}, u32[]{:S(2)}) copy-start(f32[1072]{0:T(1024)} %copy-done.36) | copy-start | bytes 12868
  479.5 186.3 %copy-start.39 = (f32[1072]{0:T(1024)S(1)}, f32[1072]{0:T(1024)}, u32[]{:S(2)}) copy-start(f32[1072]{0:T(1024)} %copy-done.38) | copy-start | bytes 12868
  479.5 186.3 %copy-start.51 = (f32[768]{0:T(1024)S(1)}, f32[768]{0:T(1024)}, u32[]{:S(2)}) copy-start(f32[768]{0:T(1024)} %copy-done.50) | copy-start | bytes 9220
  479.6 422.5 %all-gather.16.cloned.1.call-start = ((), (), s32[]{:S(2)}) async-start(), calls=%async_computation.11 | async-start | bytes 1622016 | tf_op jit(solution)/shard_map/all_gather | solution.py:242
  480.5 188.8 %copy-start.47 = (f32[1072]{0:T(1024)S(1)}, f32[1072]{0:T(1024)}, u32[]{:S(2)}) copy-start(f32[1072]{0:T(1024)} %copy-done.46) | copy-start | bytes 12868
  480.5 188.8 %copy-start.49 = (pred[1072]{0:T(1024)(128)(4,1)S(1)}, pred[1072]{0:T(1024)(128)(4,1)}, u32[]{:S(2)}) copy-start(pred[1072]{0:T(1024)(128)(4,1)} %copy-done.48) | copy-start | bytes 3220
  793.6 250.4 %reduce-scatter.13.cloned.1.call-start = ((), (), s32[]{:S(2)}) async-start(), calls=%async_computation.12 | async-start | bytes 9732096
  890.7 153.3 %copy-start.26 = (f32[768,96]{0,1:T(8,128)S(1)}, f32[768,96]{0,1:T(8,128)}, u32[]{:S(2)}) copy-start(f32[768,96]{0,1:T(8,128)} %param.19) | copy-start | bytes 884740
  890.8 153.3 %copy-start.30 = (f32[768,96]{0,1:T(8,128)S(1)}, f32[768,96]{0,1:T(8,128)}, u32[]{:S(2)}) copy-start(f32[768,96]{0,1:T(8,128)} %param.21) | copy-start | bytes 884740
  890.8 153.3 %copy-start.31 = (f32[768,96]{0,1:T(8,128)S(1)}, f32[768,96]{0,1:T(8,128)}, u32[]{:S(2)}) copy-start(f32[768,96]{0,1:T(8,128)} %param.20) | copy-start | bytes 884740
  899.2 146.8 %copy-start.32 = (f32[768,96]{0,1:T(8,128)S(1)}, f32[768,96]{0,1:T(8,128)}, u32[]{:S(2)}) copy-start(f32[768,96]{0,1:T(8,128)} %param.22) | copy-start | bytes 884740
  903.5 143.3 %copy-start.35 = (f32[13,768]{1,0:T(8,128)}, f32[13,768]{1,0:T(8,128)S(1)}, u32[]{:S(2)}) copy-start(f32[13,768]{1,0:T(8,128)S(1)} %reduce_sum.209) | copy-start | bytes 119812
  (51 other events, 344.5 us)
Sparse Core Ops, SparseCore 0:
  11.4 66.2 all-gather.7
  80.2 27.8 all-gather.11
  187.4 116.0 all-gather.9
  304.9 118.3 all-gather.13
  446.2 219.5 reduce-scatter.8
  669.7 54.8 reduce-scatter.10
  727.0 115.4 reduce-scatter.6
  846.4 55.5 all-gather.15
  909.5 134.4 reduce-scatter.12
